TPU v7x, 32 devices: a whole 2x2x4 slice. The times are simulated.
32 devices in a mesh: sph: 8 (over z, core), fit: 4 (over y, x).
Axes of the slice: x: 2, y: 2, z: 4, core: 2. Of those that a mesh axis runs over, the one named last changes fastest.
Arguments:
- tiles: bfloat16 [1024, 163840], P('fit', 'sph'), may hold values from -0.1875 to 0.1875
- coefs: bfloat16 [16, 1024], P(None, 'fit'), may hold values from -6 to 6
- centres: float32 [3, 512], P(None, ('sph', 'fit'))
- radii: float32 [512], P(('sph', 'fit')), may hold values from 1 to 1.6
- neighbours: int32 [512, 16], P(('sph', 'fit')), may hold values from 0 to 511, as said below
- counts: int32 [512], P(('sph', 'fit')), may hold values from 1 to 16
Outputs:
- moments: float32 [512, 16, 49], P(('sph', 'fit'))
- fock: float32 [16, 1024], P(None, 'fit')
Inputs may be any that keep to these rules, and one draw needn't show every extreme that they name: `neighbours`: every entry j of row i satisfies |j - i| <= 8; the first counts[i] entries of a row are distinct and differ from i, the rest equal i.
All inputs are finite; a program needn't handle non-finite values.
Results may differ from a plain program's by a relative error of at most 0.00086.
Values may be sent and summed in bfloat16 or wider, within the bound.
No kernel may reach another device: no remote copies, remote signals or barrier semaphores. Data moves between devices by JAX's collectives and lax.ppermute only.
A program may use at most 192 MiB of HBM per device.

v0:
```python
import math
import jax
import jax.numpy as jnp
from jax import lax
from jax.sharding import PartitionSpec as P

DEGREE = 6
NTH = 16
NPHI = 20
NG = 320
NDENS = 16
band = 0.1


def with_halo(array, sides, width):
    for axis, dim in sides:
        count, length = (lax.axis_size(axis), array.shape[dim])
        up = [(i, (i + 1) % count) for i in range(count - 1)]
        down = [(j, i) for i, j in up]
        last = lax.slice_in_dim(array, length - width, length, axis=dim)
        initial = lax.slice_in_dim(array, 0, width, axis=dim)
        before = lax.ppermute(last, axis, up)
        after = lax.ppermute(initial, axis, down)
        array = jnp.concatenate([before, array, after], axis=dim)
    return array


def solid(coord_x, coord_y, coord_z):
    radius_squared = coord_x * coord_x + coord_y * coord_y + coord_z * coord_z
    cos_part = [jnp.ones_like(coord_x)]
    sin_part = [jnp.zeros_like(coord_x)]
    for harmonic_order in range(1, DEGREE + 1):
        cprev = cos_part[-1]
        sprev = sin_part[-1]
        cos_part.append(cprev * coord_x - sprev * coord_y)
        sin_part.append(cprev * coord_y + sprev * coord_x)
    result = [None] * (DEGREE + 1) ** 2
    for harmonic_order in range(DEGREE + 1):
        dfact = 1.0
        for odd in range(1, 2 * harmonic_order, 2):
            dfact = dfact * odd
        lower_term = None
        current = dfact * jnp.ones_like(coord_x)
        for harmonic_degree in range(harmonic_order, DEGREE + 1):
            if harmonic_degree > harmonic_order:
                next_term = (2 * harmonic_degree - 1) * coord_z * current
                if lower_term is not None:
                    next_term = (
                        next_term
                        - (harmonic_degree + harmonic_order - 1) * radius_squared * lower_term
                    )
                lower_term = current
                current = next_term / (harmonic_degree - harmonic_order)
            scale = math.sqrt(
                (2 * harmonic_degree + 1)
                / (4 * math.pi)
                * math.factorial(harmonic_degree - harmonic_order)
                / math.factorial(harmonic_degree + harmonic_order)
            )
            if harmonic_order == 0:
                result[harmonic_degree * harmonic_degree + harmonic_degree] = scale * current
            else:
                result[harmonic_degree * harmonic_degree + harmonic_degree + harmonic_order] = (
                    math.sqrt(2.0) * scale * current * cos_part[harmonic_order]
                )
                result[harmonic_degree * harmonic_degree + harmonic_degree - harmonic_order] = (
                    math.sqrt(2.0) * scale * current * sin_part[harmonic_order]
                )
    return result


def grid_tables():
    polar_index = jnp.arange(NTH, dtype=jnp.float32)
    polar_nodes = -1.0 + (2.0 * polar_index + 1.0) / NTH
    angles = (jnp.arange(NPHI, dtype=jnp.float32) + 0.5) * (2.0 * math.pi / NPHI)
    cosines = jnp.repeat(polar_nodes, NPHI)
    sines = jnp.sqrt(1.0 - cosines * cosines)
    azimuth = jnp.tile(angles, NTH)
    dirs = jnp.stack([sines * jnp.cos(azimuth), sines * jnp.sin(azimuth), cosines])
    weights = jnp.full((NTH * NPHI,), 4.0 * math.pi / (NTH * NPHI), dtype=jnp.float32)
    ysurf = jnp.stack(solid(dirs[0], dirs[1], dirs[2]))
    levels = jnp.asarray(
        [
            float(harmonic_degree)
            for harmonic_degree in range(DEGREE + 1)
            for harmonic_order in range(2 * harmonic_degree + 1)
        ],
        dtype=jnp.float32,
    )
    couple = 4.0 * math.pi / (2.0 * levels + 1.0)
    invert = (2.0 * levels + 1.0) / (4.0 * math.pi)
    return (dirs, weights, ysurf, couple, invert)


def block_basis(own, near, valid, dirs, couple):
    centre = own[:3]
    radius = own[3]
    offset = centre[:, :, None] - near[:3]
    near_rad = jnp.where(valid > 0, near[3], 1.0)
    vec = (offset[:, :, :, None] + radius[None, :, None, None] * dirs[:, None, None, :]) / near_rad[
        None, :, :, None
    ]
    dist = jnp.sqrt(jnp.sum(vec * vec, axis=0))
    ramp = jnp.clip((1.0 - dist) / band, 0.0, 1.0)
    switch = ramp * ramp * (3.0 - 2.0 * ramp) * valid[:, :, None]
    harm = jnp.stack(solid(vec[0], vec[1], vec[2]), axis=2)
    basis = harm * couple[None, None, :, None] * switch[:, :, None, :]
    uncovered = jnp.maximum(0.0, 1.0 - jnp.sum(switch, axis=1))
    return (basis, uncovered)


def block_rhs(weighted, uncovered, potential):
    return -jnp.einsum(
        "lp,sdp->sdl", weighted, uncovered[:, None, :] * potential, precision=lax.Precision.HIGHEST
    )


def block_sweep(basis, weighted, invert, rhs, near_moments):
    field = jnp.einsum("sklp,skdl->sdp", basis, near_moments, precision=lax.Precision.HIGHEST)
    proj = jnp.einsum("lp,sdp->sdl", weighted, field, precision=lax.Precision.HIGHEST)
    return invert[None, None, :] * (rhs + proj)


def block_charges(ysurf, weights, uncovered, moments):
    surface = jnp.einsum("lp,sdl->sdp", ysurf, moments, precision=lax.Precision.HIGHEST)
    return (surface * (weights[None, None, :] * uncovered[:, None, :])).astype(jnp.bfloat16)


def body(tiles, coefs, centres, radii, neighbours, counts):
    spheres = neighbours.shape[0]
    slots = neighbours.shape[1]
    reach = slots // 2
    aux_local = tiles.shape[0]
    block = tiles.shape[1] // NG
    dirs, weights, ysurf, couple, invert = grid_tables()
    weighted = ysurf * weights[None, :]
    tile_three = tiles.reshape(aux_local, block, NG)
    fit_index = lax.axis_index("fit")
    first_sphere = (lax.axis_index("sph") * lax.axis_size("fit") + fit_index) * spheres
    whole = jnp.einsum("da,acn->cdn", coefs, tile_three, preferred_element_type=jnp.float32)
    whole = lax.psum(whole.reshape(block, NDENS * NG), "fit")
    potential = lax.dynamic_slice_in_dim(whole, fit_index * spheres, spheres, 0)
    potential = potential.reshape(spheres, NDENS, NG)
    geometry = jnp.concatenate([centres, radii[None, :]], axis=0)
    valid = (jnp.arange(slots)[None, :] < counts[:, None]).astype(jnp.float32)
    near_geo = with_halo(geometry, ((("sph", "fit"), 1),), reach)
    local = jnp.clip(neighbours - (first_sphere - reach), 0, spheres + 2 * reach - 1)
    basis, uncovered = block_basis(geometry, near_geo[:, local], valid, dirs, couple)
    rhs = block_rhs(weighted, uncovered, potential)
    moments = invert[None, None, :] * rhs
    for sweep in range(2):
        near_state = with_halo(moments, ((("sph", "fit"), 0),), reach)
        moments = block_sweep(basis, weighted, invert, rhs, near_state[local])
    charges = block_charges(ysurf, weights, uncovered, moments).reshape(spheres, NDENS * NG)
    piece = lax.all_gather(charges, "fit", axis=0, tiled=True)
    rows = piece.shape[0]
    shaped = piece.reshape(rows, NDENS, NG)
    partial_fock = lax.dot_general(
        shaped, tile_three, (((0, 2), (1, 2)), ((), ())), preferred_element_type=jnp.float32
    )
    fock = lax.psum(partial_fock, "sph")
    return (moments, fock)


def solution(mesh):
    placed = (
        P("fit", "sph"),
        P(None, "fit"),
        P(None, ("sph", "fit")),
        P(("sph", "fit")),
        P(("sph", "fit"), None),
        P(("sph", "fit")),
    )
    return jax.shard_map(
        body,
        mesh=mesh,
        in_specs=placed,
        out_specs=(P(("sph", "fit"), None, None), P(None, "fit")),
        check_vma=False,
    )
```

profile of v0, /device:TPU:0, one launch (start us, length us, event | category | flops | bytes accessed | tf_op | source)
XLA Modules:
  0.0 242.6 jit_solution(9293991548820046019)
XLA Ops:
  8.0 4.8 %collective-permute-start = (f32[4,8]{1,0:T(4,128)S(1)}, f32[4,8]{1,0:T(4,128)S(1)}, u32[]{:S(2)}, u32[]{:S(2)}) collective-permute-start(f32[4,8]{1,0:T(4,128)S(1)} %get-tuple-element.90), channel_id=1, source_target_pairs={{0,1},{1,2},{2,3},{3,4},{4,5},{5,6},{6,7},{7,8},{8,9},{9,10},{10,1... | collective-permute-start | bytes 392 | tf_op jit(solution)/shard_map/ppermute | solution.py:22
  12.9 1.4 collective-permute-start.1
  14.3 13.7 %copy.25 = bf16[256,20480]{0,1:T(8,128)(2,1)} copy(bf16[256,20480]{1,0:T(8,128)(2,1)} %param.7) | data formatting | bytes 20971520 | tf_op args[0]
  28.0 7.1 %convolution_bitcast_fusion = f32[64,16,320]{2,1,0:T(8,128)S(1)} fusion(bf16[256,64,320]{0,2,1:T(8,128)(2,1)} %bitcast.208, bf16[16,256]{1,0:T(8,128)(2,1)S(1)} %copy-done), kind=kOutput, calls=%fused_computation.8 | convolution fusion | flops 167772160 | bytes 11804672 | tf_op jit(solution)/shard_map/da,acn->cdn/dot_general | solution.py:140
  35.1 1.6 reshape.3985
  40.2 0.9 multiply_dynamic-update-slice_fusion.47
  41.8 0.8 multiply_dynamic-update-slice_fusion.45
  42.7 0.9 multiply_dynamic-update-slice_fusion.44
  43.6 0.8 multiply_dynamic-update-slice_fusion.43
  44.4 0.9 multiply_dynamic-update-slice_fusion.42
  45.3 0.8 multiply_dynamic-update-slice_fusion.41
  46.2 0.9 multiply_dynamic-update-slice_fusion.40
  47.0 0.9 multiply_dynamic-update-slice_fusion.39
  47.9 0.9 multiply_dynamic-update-slice_fusion.38
  48.8 0.9 multiply_dynamic-update-slice_fusion.37
  49.7 0.9 multiply_dynamic-update-slice_fusion.36
  50.5 0.8 multiply_dynamic-update-slice_fusion.35
  52.2 0.9 multiply_dynamic-update-slice_fusion.33
  53.1 0.9 multiply_dynamic-update-slice_fusion.32
  54.7 0.9 multiply_dynamic-update-slice_fusion.30
  55.7 0.9 multiply_dynamic-update-slice_fusion.29
  56.6 1.0 multiply_dynamic-update-slice_fusion.28
  57.6 1.0 multiply_dynamic-update-slice_fusion.27
  58.5 0.9 multiply_dynamic-update-slice_fusion.26
  59.4 0.8 multiply_dynamic-update-slice_fusion.25
  60.2 0.9 multiply_dynamic-update-slice_fusion.24
  61.1 0.9 multiply_dynamic-update-slice_fusion.23
  62.0 0.8 multiply_dynamic-update-slice_fusion.22
  62.8 0.9 multiply_dynamic-update-slice_fusion.21
  63.7 0.9 multiply_dynamic-update-slice_fusion.20
  64.6 1.0 multiply_dynamic-update-slice_fusion.19
  65.7 1.1 multiply_dynamic-update-slice_fusion.18
  66.7 1.1 multiply_dynamic-update-slice_fusion.17
  67.8 0.9 multiply_dynamic-update-slice_fusion.16
  68.7 0.9 multiply_dynamic-update-slice_fusion.15
  69.6 0.8 multiply_dynamic-update-slice_fusion.14
  70.4 0.9 multiply_dynamic-update-slice_fusion.13
  71.3 0.8 multiply_dynamic-update-slice_fusion.12
  72.9 0.9 multiply_dynamic-update-slice_fusion.10
  73.8 0.9 multiply_dynamic-update-slice_fusion.9
  74.8 1.0 multiply_dynamic-update-slice_fusion.8
  75.8 1.1 multiply_dynamic-update-slice_fusion.7
  76.9 1.1 multiply_dynamic-update-slice_fusion.6
  78.0 1.1 multiply_dynamic-update-slice_fusion.5
  79.4 1.0 multiply_dynamic-update-slice_fusion.4
  80.4 0.9 multiply_dynamic-update-slice_fusion.3
  81.4 0.8 multiply_dynamic-update-slice_fusion.2
  82.2 0.8 multiply_dynamic-update-slice_fusion.1
  83.1 0.9 multiply_dynamic-update-slice_fusion
  83.9 11.8 %all-reduce.2.cloned.1.call-done = f32[64,5120]{1,0:T(8,128)} async-done(((f32[64,5120]{1,0:T(8,128)}), f32[64,5120]{1,0:T(8,128)}) %all-reduce.2.cloned.1.call-update) | async-done | bytes 1310736 | tf_op jit(solution)/shard_map/psum | solution.py:141
  95.7 1.0 constant_dynamic-slice_fusion
  97.4 3.4 %collective-permute-start.2 = (f32[8,16,49]{2,1,0:T(8,128)S(1)}, f32[8,16,49]{2,1,0:T(8,128)S(1)}, u32[]{:S(2)}, u32[]{:S(2)}) collective-permute-start(f32[8,16,49]{2,1,0:T(8,128)S(1)} %get-tuple-element.58), channel_id=1, source_target_pairs={{0,1},{1,2},{2,3},{3,4},{4,5},{5,6},{6,7},{7,8},{8,9},{9,10},{10,1... | collective-permute-start | bytes 75272 | tf_op jit(solution)/shard_map/ppermute | solution.py:22
  100.7 1.5 collective-permute-start.3
  102.2 15.1 %multiply_multiply_fusion = f32[16,16,49,320]{3,1,2,0:T(8,128)} fusion(f32[16,16,49,320]{3,1,2,0:T(8,128)} %multiply_dynamic-update-slice_fusion, f32[16,16,320]{2,1,0:T(8,128)S(1)} %get-tuple-element.55, f32[49]{0:T(128)S(1)} %copy-done.8), kind=kLoop, calls=%fused_computation.7 | loop fusion | flops 8028160 | bytes 32440516 | tf_op jit(solution)/shard_map/mul | solution.py:107
  117.4 1.0 gather_fusion.1
  118.4 28.6 %fusion.4 = f32[16,16,320]{2,1,0:T(8,128)S(1)} fusion(f32[16,16,16,49]{3,2,1,0:T(8,128)S(1)} %bitcast.211, f32[16,16,49,320]{3,1,2,0:T(8,128)} %multiply_multiply_fusion), kind=kOutput, calls=%fused_computation.10 | convolution fusion | flops 770703360 | bytes 17186816 | tf_op jit(solution)/shard_map/sklp,skdl->sdp/dot_general | solution.py:119
  147.5 4.5 %collective-permute-start.4 = (f32[8,16,49]{2,1,0:T(8,128)S(1)}, f32[8,16,49]{2,1,0:T(8,128)S(1)}, u32[]{:S(2)}, u32[]{:S(2)}) collective-permute-start(f32[8,16,49]{2,1,0:T(8,128)S(1)} %get-tuple-element.56), channel_id=1, source_target_pairs={{0,1},{1,2},{2,3},{3,4},{4,5},{5,6},{6,7},{7,8},{8,9},{9,10},{10,1... | collective-permute-start | bytes 75272 | tf_op jit(solution)/shard_map/ppermute | solution.py:22
  152.1 1.5 collective-permute-start.5
  153.9 4.6 %collective-permute-done.5 = f32[8,16,49]{2,1,0:T(8,128)S(1)} collective-permute-done((f32[8,16,49]{2,1,0:T(8,128)S(1)}, f32[8,16,49]{2,1,0:T(8,128)S(1)}, u32[]{:S(2)}, u32[]{:S(2)}) %collective-permute-start.5) | collective-permute-done | bytes 25120 | tf_op jit(solution)/shard_map/ppermute | solution.py:23
  158.5 1.0 gather_fusion.2
  159.6 28.6 %fusion.7 = f32[16,16,320]{2,1,0:T(8,128)S(1)} fusion(f32[16,16,16,49]{3,2,1,0:T(8,128)S(1)} %bitcast.210, f32[16,16,49,320]{3,1,2,0:T(8,128)} %multiply_multiply_fusion), kind=kOutput, calls=%fused_computation.11 | convolution fusion | flops 770703360 | bytes 17186816 | tf_op jit(solution)/shard_map/sklp,skdl->sdp/dot_general | solution.py:119
  189.3 13.8 %all_gather.3 = bf16[64,5120]{1,0:T(8,128)(2,1)S(1)} all-gather(bf16[16,5120]{1,0:T(8,128)(2,1)S(1)} %reshape.3987), channel_id=1, replica_groups=mesh['sph'=8,'fit'=4] {'fit'}, dimensions={0}, use_global_device_ids=true | all-gather | bytes 819200 | tf_op jit(solution)/shard_map/all_gather | solution.py:155
  203.7 5.5 %convolution_bitcast_fusion.1 = f32[16,256]{1,0:T(8,128)S(1)} fusion(bf16[64,16,320]{2,1,0:T(8,128)(2,1)S(1)} %reshape.3988, bf16[256,64,320]{0,2,1:T(8,128)(2,1)} %bitcast.209), kind=kOutput, calls=%fused_computation.20 | convolution fusion | flops 167772160 | bytes 11157504 | tf_op jit(solution)/shard_map/dot_general | solution.py:158
  209.2 26.5 %psum.15 = f32[16,256]{1,0:T(8,128)} all-reduce(f32[16,256]{1,0:T(8,128)S(1)} %convolution_bitcast_fusion.1), channel_id=1, replica_groups=mesh['sph'=8,'fit'=4] {'sph'}, use_global_device_ids=true, to_apply=%region_3.4 | all-reduce | flops 4096 | bytes 32768 | tf_op jit(solution)/shard_map/psum | solution.py:161
  (77 shorter events, 11.0 us)
Async XLA Ops:
  7.2 20.8 %copy-start = (bf16[16,256]{1,0:T(8,128)(2,1)S(1)}, bf16[16,256]{1,0:T(8,128)(2,1)}, u32[]{:S(2)}) copy-start(bf16[16,256]{1,0:T(8,128)(2,1)} %param.8) | copy-start | bytes 24580
  7.2 88.5 %all-reduce.2.cloned.1.call-start = ((), (), s32[]{:S(2)}) async-start(), calls=%async_computation | async-start | bytes 2621440 | tf_op jit(solution)/shard_map/psum | solution.py:141
  8.0 30.6 %collective-permute-start = (f32[4,8]{1,0:T(4,128)S(1)}, f32[4,8]{1,0:T(4,128)S(1)}, u32[]{:S(2)}, u32[]{:S(2)}) collective-permute-start(f32[4,8]{1,0:T(4,128)S(1)} %get-tuple-element.90), channel_id=1, source_target_pairs={{0,1},{1,2},{2,3},{3,4},{4,5},{5,6},{6,7},{7,8},{8,9},{9,10},{10,1... | collective-permute-start | bytes 392 | tf_op jit(solution)/shard_map/ppermute | solution.py:22
  12.8 25.1 %copy-start.5 = (f32[16]{0:T(128)S(1)}, f32[16]{0:T(128)}, u32[]{:S(2)}) copy-start(f32[16]{0:T(128)} %param.10) | copy-start | bytes 196
  12.9 25.2 %copy-start.4 = (s32[16,16]{1,0:T(8,128)S(1)}, s32[16,16]{1,0:T(8,128)}, u32[]{:S(2)}) copy-start(s32[16,16]{1,0:T(8,128)} %param.11) | copy-start | bytes 3076
  12.9 25.3 %copy-start.7 = (s32[16]{0:T(128)S(1)}, s32[16]{0:T(128)}, u32[]{:S(2)}) copy-start(s32[16]{0:T(128)} %param.12) | copy-start | bytes 196
  12.9 25.8 %copy-start.3 = (f32[3,16]{1,0:T(4,128)S(1)}, f32[3,16]{1,0:T(4,128)}, u32[]{:S(2)}) copy-start(f32[3,16]{1,0:T(4,128)} %param.9) | copy-start | bytes 580
  12.9 25.7 %collective-permute-start.1 = (f32[4,8]{1,0:T(4,128)S(1)}, f32[4,8]{1,0:T(4,128)S(1)}, u32[]{:S(2)}, u32[]{:S(2)}) collective-permute-start(f32[4,8]{1,0:T(4,128)S(1)} %get-tuple-element.91), channel_id=1, source_target_pairs={{1,0},{2,1},{3,2},{4,3},{5,4},{6,5},{7,6},{8,7},{9,8},{10,9},{11,1... | collective-permute-start | bytes 392 | tf_op jit(solution)/shard_map/ppermute | solution.py:23
  62.0 34.9 %copy-start.6 = (f32[49]{0:T(128)S(1)}, f32[49]{0:T(128)}, u32[]{:S(2)}) copy-start(f32[49]{0:T(128)} %constant.272) | copy-start | bytes 592
  62.0 40.3 %copy-start.8 = (f32[49]{0:T(128)S(1)}, f32[49]{0:T(128)}, u32[]{:S(2)}) copy-start(f32[49]{0:T(128)} %constant.273) | copy-start | bytes 592
  97.4 20.0 %collective-permute-start.2 = (f32[8,16,49]{2,1,0:T(8,128)S(1)}, f32[8,16,49]{2,1,0:T(8,128)S(1)}, u32[]{:S(2)}, u32[]{:S(2)}) collective-permute-start(f32[8,16,49]{2,1,0:T(8,128)S(1)} %get-tuple-element.58), channel_id=1, source_target_pairs={{0,1},{1,2},{2,3},{3,4},{4,5},{5,6},{6,7},{7,8},{8,9},{9,10},{10,1... | collective-permute-start | bytes 75272 | tf_op jit(solution)/shard_map/ppermute | solution.py:22
  100.7 16.6 %collective-permute-start.3 = (f32[8,16,49]{2,1,0:T(8,128)S(1)}, f32[8,16,49]{2,1,0:T(8,128)S(1)}, u32[]{:S(2)}, u32[]{:S(2)}) collective-permute-start(f32[8,16,49]{2,1,0:T(8,128)S(1)} %get-tuple-element.59), channel_id=1, source_target_pairs={{1,0},{2,1},{3,2},{4,3},{5,4},{6,5},{7,6},{8,7},{9,8},{10,9},{11,1... | collective-permute-start | bytes 75272 | tf_op jit(solution)/shard_map/ppermute | solution.py:23
  147.5 6.4 %collective-permute-start.4 = (f32[8,16,49]{2,1,0:T(8,128)S(1)}, f32[8,16,49]{2,1,0:T(8,128)S(1)}, u32[]{:S(2)}, u32[]{:S(2)}) collective-permute-start(f32[8,16,49]{2,1,0:T(8,128)S(1)} %get-tuple-element.56), channel_id=1, source_target_pairs={{0,1},{1,2},{2,3},{3,4},{4,5},{5,6},{6,7},{7,8},{8,9},{9,10},{10,1... | collective-permute-start | bytes 75272 | tf_op jit(solution)/shard_map/ppermute | solution.py:22
  152.1 6.4 %collective-permute-start.5 = (f32[8,16,49]{2,1,0:T(8,128)S(1)}, f32[8,16,49]{2,1,0:T(8,128)S(1)}, u32[]{:S(2)}, u32[]{:S(2)}) collective-permute-start(f32[8,16,49]{2,1,0:T(8,128)S(1)} %get-tuple-element.57), channel_id=1, source_target_pairs={{1,0},{2,1},{3,2},{4,3},{5,4},{6,5},{7,6},{8,7},{9,8},{10,9},{11,1... | collective-permute-start | bytes 75272 | tf_op jit(solution)/shard_map/ppermute | solution.py:23
  159.5 76.2 %copy-start.1 = (bf16[16,256]{1,0:T(8,128)(2,1)S(1)}, bf16[16,256]{1,0:T(8,128)(2,1)}, u32[]{:S(2)}) copy-start(bf16[16,256]{1,0:T(8,128)(2,1)} %param.8) | copy-start | bytes 24580
  188.6 47.1 %copy-start.2 = (f32[16,16,49]{2,1,0:T(8,128)}, f32[16,16,49]{2,1,0:T(8,128)S(1)}, u32[]{:S(2)}) copy-start(f32[16,16,49]{2,1,0:T(8,128)S(1)} %fusion.11) | copy-start | bytes 150532
Sparse Core Ops, SparseCore 0:
  36.8 58.9 all-reduce.1
where the time goes:
time: 243 us
  matrix products  71.6 us (29%)
  other arithmetic  60.6 us (25%)
  blocking collectives  40.3 us (17%)
  local copies, waits for them, and re-layouts  21.7 us (9%)
  starting transfers between devices  17.2 us (7%)
  waiting for transfers between devices  16.7 us (7%)
  between operations  14.4 us (6%)
    dot_general x2, matrix products, block_sweep(): jnp.einsum('sklp,skdl->sdp', basis, near_moments, precision=lax.Precision...  57.2 us
    unnamed x47, other arithmetic  42.6 us
    psum x1, blocking collectives, body(): fock = lax.psum(partial_fock, 'sph')  26.5 us
    mul x1, other arithmetic, block_basis(): basis = harm * couple[None, None, :, None] * switch[:, :, None, :]  15.1 us
    unnamed x20, local copies, waits for them, and re-layouts  14.5 us
    all_gather x1, blocking collectives, body(): piece = lax.all_gather(charges, 'fit', axis=0, tiled=True)  13.8 us
    ppermute x3, starting transfers between devices, with_halo(): before = lax.ppermute(last, axis, up)  12.8 us
    psum x1, waiting for transfers between devices, body(): whole = lax.psum(whole.reshape(block, NDENS * NG), 'fit')  11.8 us
  transfers between devices with their start and end apart: 7, of which 3 were waited for; matrix products, arithmetic and copies ran while one was open for 35% of the time, Pallas kernels for 0%

commit v1 on v0

--- a/solution.py
+++ b/solution.py
@@ -158,7 +158,7 @@
     partial_fock = lax.dot_general(
         shaped, tile_three, (((0, 2), (1, 2)), ((), ())), preferred_element_type=jnp.float32
     )
-    fock = lax.psum(partial_fock, "sph")
+    fock = jnp.sum(lax.all_gather(partial_fock, "sph"), axis=0)
     return (moments, fock)
 
 

time: 243 us -> 232 us (0.955)
  blocking collectives: 40.3 us -> 27.8 us
    psum x1 -> x0, blocking collectives: 26.5 us -> none  [body(): fock = lax.psum(partial_fock, 'sph')]
    all_gather x0 -> x1, blocking collectives: none -> 14 us  [body(): fock = jnp.sum(lax.all_gather(partial_fock, 'sph'), axis=0)]
  transfers between devices with their start and end apart: 7 -> 7, of which waited for: 3 -> 3; matrix products, arithmetic and copies ran while one was open for 35% -> 37% of each run, Pallas kernels for 0% -> 0%
where the time goes in v1:
time: 232 us; the launch traced here: 231 us
  matrix products  71.6 us (31%)
  other arithmetic  61.2 us (26%)
  blocking collectives  27.8 us (12%)
  local copies, waits for them, and re-layouts  21.7 us (9%)
  starting transfers between devices  17.2 us (7%)
  waiting for transfers between devices  16.7 us (7%)
  between operations  14.4 us (6%)
    dot_general x2, matrix products, block_sweep(): jnp.einsum('sklp,skdl->sdp', basis, near_moments, precision=lax.Precision...  57.2 us
    unnamed x47, other arithmetic  42.6 us
    mul x1, other arithmetic, block_basis(): basis = harm * couple[None, None, :, None] * switch[:, :, None, :]  15.1 us
    unnamed x20, local copies, waits for them, and re-layouts  14.5 us
    all_gather x1, blocking collectives, body(): fock = jnp.sum(lax.all_gather(partial_fock, 'sph'), axis=0)  14 us
    all_gather x1, blocking collectives, body(): piece = lax.all_gather(charges, 'fit', axis=0, tiled=True)  13.8 us
    ppermute x3, starting transfers between devices, with_halo(): before = lax.ppermute(last, axis, up)  12.8 us
    psum x1, waiting for transfers between devices, body(): whole = lax.psum(whole.reshape(block, NDENS * NG), 'fit')  11.8 us
  transfers between devices with their start and end apart: 7, of which 3 were waited for; matrix products, arithmetic and copies ran while one was open for 37% of the time, Pallas kernels for 0%

profile of v1, /device:TPU:0, one launch (start us, length us, event | category | flops | bytes accessed | tf_op | source)
XLA Modules:
  0.0 230.7 jit_solution(10894861587481746320)
XLA Ops:
  8.0 4.8 %collective-permute-start = (f32[4,8]{1,0:T(4,128)S(1)}, f32[4,8]{1,0:T(4,128)S(1)}, u32[]{:S(2)}, u32[]{:S(2)}) collective-permute-start(f32[4,8]{1,0:T(4,128)S(1)} %get-tuple-element.90), channel_id=1, source_target_pairs={{0,1},{1,2},{2,3},{3,4},{4,5},{5,6},{6,7},{7,8},{8,9},{9,10},{10,1... | collective-permute-start | bytes 392 | tf_op jit(solution)/shard_map/ppermute | solution.py:22
  12.9 1.4 collective-permute-start.1
  14.3 13.7 %copy.25 = bf16[256,20480]{0,1:T(8,128)(2,1)} copy(bf16[256,20480]{1,0:T(8,128)(2,1)} %param.7) | data formatting | bytes 20971520 | tf_op args[0]
  28.0 7.1 %convolution_bitcast_fusion = f32[64,16,320]{2,1,0:T(8,128)S(1)} fusion(bf16[256,64,320]{0,2,1:T(8,128)(2,1)} %bitcast.209, bf16[16,256]{1,0:T(8,128)(2,1)S(1)} %copy-done), kind=kOutput, calls=%fused_computation.8 | convolution fusion | flops 167772160 | bytes 11804672 | tf_op jit(solution)/shard_map/da,acn->cdn/dot_general | solution.py:140
  35.1 1.6 reshape.3985
  40.2 0.9 multiply_dynamic-update-slice_fusion.47
  41.8 0.8 multiply_dynamic-update-slice_fusion.45
  42.7 0.9 multiply_dynamic-update-slice_fusion.44
  43.6 0.8 multiply_dynamic-update-slice_fusion.43
  44.4 0.9 multiply_dynamic-update-slice_fusion.42
  45.3 0.8 multiply_dynamic-update-slice_fusion.41
  46.2 0.9 multiply_dynamic-update-slice_fusion.40
  47.0 0.9 multiply_dynamic-update-slice_fusion.39
  47.9 0.9 multiply_dynamic-update-slice_fusion.38
  48.8 0.9 multiply_dynamic-update-slice_fusion.37
  49.7 0.9 multiply_dynamic-update-slice_fusion.36
  50.5 0.8 multiply_dynamic-update-slice_fusion.35
  52.2 0.9 multiply_dynamic-update-slice_fusion.33
  53.1 0.9 multiply_dynamic-update-slice_fusion.32
  54.7 0.9 multiply_dynamic-update-slice_fusion.30
  55.7 0.9 multiply_dynamic-update-slice_fusion.29
  56.6 1.0 multiply_dynamic-update-slice_fusion.28
  57.6 1.0 multiply_dynamic-update-slice_fusion.27
  58.5 0.9 multiply_dynamic-update-slice_fusion.26
  59.4 0.8 multiply_dynamic-update-slice_fusion.25
  60.2 0.9 multiply_dynamic-update-slice_fusion.24
  61.1 0.9 multiply_dynamic-update-slice_fusion.23
  62.0 0.8 multiply_dynamic-update-slice_fusion.22
  62.8 0.9 multiply_dynamic-update-slice_fusion.21
  63.7 0.9 multiply_dynamic-update-slice_fusion.20
  64.6 1.0 multiply_dynamic-update-slice_fusion.19
  65.7 1.1 multiply_dynamic-update-slice_fusion.18
  66.7 1.1 multiply_dynamic-update-slice_fusion.17
  67.8 0.9 multiply_dynamic-update-slice_fusion.16
  68.7 0.9 multiply_dynamic-update-slice_fusion.15
  69.6 0.8 multiply_dynamic-update-slice_fusion.14
  70.4 0.9 multiply_dynamic-update-slice_fusion.13
  71.3 0.8 multiply_dynamic-update-slice_fusion.12
  72.9 0.9 multiply_dynamic-update-slice_fusion.10
  73.8 0.9 multiply_dynamic-update-slice_fusion.9
  74.8 1.0 multiply_dynamic-update-slice_fusion.8
  75.8 1.1 multiply_dynamic-update-slice_fusion.7
  76.9 1.1 multiply_dynamic-update-slice_fusion.6
  78.0 1.1 multiply_dynamic-update-slice_fusion.5
  79.4 1.0 multiply_dynamic-update-slice_fusion.4
  80.4 0.9 multiply_dynamic-update-slice_fusion.3
  81.4 0.8 multiply_dynamic-update-slice_fusion.2
  82.2 0.8 multiply_dynamic-update-slice_fusion.1
  83.1 0.9 multiply_dynamic-update-slice_fusion
  83.9 11.8 %all-reduce.2.cloned.1.call-done = f32[64,5120]{1,0:T(8,128)} async-done(((f32[64,5120]{1,0:T(8,128)}), f32[64,5120]{1,0:T(8,128)}) %all-reduce.2.cloned.1.call-update) | async-done | bytes 1310736 | tf_op jit(solution)/shard_map/psum | solution.py:141
  95.7 1.0 constant_dynamic-slice_fusion
  97.4 3.4 %collective-permute-start.2 = (f32[8,16,49]{2,1,0:T(8,128)S(1)}, f32[8,16,49]{2,1,0:T(8,128)S(1)}, u32[]{:S(2)}, u32[]{:S(2)}) collective-permute-start(f32[8,16,49]{2,1,0:T(8,128)S(1)} %get-tuple-element.58), channel_id=1, source_target_pairs={{0,1},{1,2},{2,3},{3,4},{4,5},{5,6},{6,7},{7,8},{8,9},{9,10},{10,1... | collective-permute-start | bytes 75272 | tf_op jit(solution)/shard_map/ppermute | solution.py:22
  100.7 1.5 collective-permute-start.3
  102.2 15.1 %multiply_multiply_fusion = f32[16,16,49,320]{3,1,2,0:T(8,128)} fusion(f32[16,16,49,320]{3,1,2,0:T(8,128)} %multiply_dynamic-update-slice_fusion, f32[16,16,320]{2,1,0:T(8,128)S(1)} %get-tuple-element.55, f32[49]{0:T(128)S(1)} %copy-done.8), kind=kLoop, calls=%fused_computation.7 | loop fusion | flops 8028160 | bytes 32440516 | tf_op jit(solution)/shard_map/mul | solution.py:107
  117.4 1.0 gather_fusion.1
  118.4 28.6 %fusion.4 = f32[16,16,320]{2,1,0:T(8,128)S(1)} fusion(f32[16,16,16,49]{3,2,1,0:T(8,128)S(1)} %bitcast.212, f32[16,16,49,320]{3,1,2,0:T(8,128)} %multiply_multiply_fusion), kind=kOutput, calls=%fused_computation.10 | convolution fusion | flops 770703360 | bytes 17186816 | tf_op jit(solution)/shard_map/sklp,skdl->sdp/dot_general | solution.py:119
  147.5 4.5 %collective-permute-start.4 = (f32[8,16,49]{2,1,0:T(8,128)S(1)}, f32[8,16,49]{2,1,0:T(8,128)S(1)}, u32[]{:S(2)}, u32[]{:S(2)}) collective-permute-start(f32[8,16,49]{2,1,0:T(8,128)S(1)} %get-tuple-element.56), channel_id=1, source_target_pairs={{0,1},{1,2},{2,3},{3,4},{4,5},{5,6},{6,7},{7,8},{8,9},{9,10},{10,1... | collective-permute-start | bytes 75272 | tf_op jit(solution)/shard_map/ppermute | solution.py:22
  152.1 1.5 collective-permute-start.5
  153.9 4.6 %collective-permute-done.5 = f32[8,16,49]{2,1,0:T(8,128)S(1)} collective-permute-done((f32[8,16,49]{2,1,0:T(8,128)S(1)}, f32[8,16,49]{2,1,0:T(8,128)S(1)}, u32[]{:S(2)}, u32[]{:S(2)}) %collective-permute-start.5) | collective-permute-done | bytes 25120 | tf_op jit(solution)/shard_map/ppermute | solution.py:23
  158.5 1.0 gather_fusion.2
  159.6 28.6 %fusion.7 = f32[16,16,320]{2,1,0:T(8,128)S(1)} fusion(f32[16,16,16,49]{3,2,1,0:T(8,128)S(1)} %bitcast.211, f32[16,16,49,320]{3,1,2,0:T(8,128)} %multiply_multiply_fusion), kind=kOutput, calls=%fused_computation.11 | convolution fusion | flops 770703360 | bytes 17186816 | tf_op jit(solution)/shard_map/sklp,skdl->sdp/dot_general | solution.py:119
  189.3 13.8 %all_gather.9 = bf16[64,5120]{1,0:T(8,128)(2,1)S(1)} all-gather(bf16[16,5120]{1,0:T(8,128)(2,1)S(1)} %reshape.3987), channel_id=1, replica_groups=mesh['sph'=8,'fit'=4] {'fit'}, dimensions={0}, use_global_device_ids=true | all-gather | bytes 819200 | tf_op jit(solution)/shard_map/all_gather | solution.py:155
  203.7 5.5 %convolution_bitcast_fusion.1 = f32[16,256]{1,0:T(8,128)S(1)} fusion(bf16[64,16,320]{2,1,0:T(8,128)(2,1)S(1)} %reshape.3988, bf16[256,64,320]{0,2,1:T(8,128)(2,1)} %bitcast.210), kind=kOutput, calls=%fused_computation.20 | convolution fusion | flops 167772160 | bytes 11157504 | tf_op jit(solution)/shard_map/dot_general | solution.py:158
  209.2 14.0 %all-gather = f32[128,256]{1,0:T(8,128)S(1)} all-gather(f32[16,256]{1,0:T(8,128)S(1)} %convolution_bitcast_fusion.1), channel_id=2, replica_groups=mesh['sph'=8,'fit'=4] {'sph'}, dimensions={0}, use_global_device_ids=true | all-gather | bytes 147456 | tf_op jit(solution)/shard_map/all_gather | solution.py:161
  (78 shorter events, 11.6 us)
Async XLA Ops:
  7.2 20.8 %copy-start = (bf16[16,256]{1,0:T(8,128)(2,1)S(1)}, bf16[16,256]{1,0:T(8,128)(2,1)}, u32[]{:S(2)}) copy-start(bf16[16,256]{1,0:T(8,128)(2,1)} %param.8) | copy-start | bytes 24580
  7.2 88.5 %all-reduce.2.cloned.1.call-start = ((), (), s32[]{:S(2)}) async-start(), calls=%async_computation | async-start | bytes 2621440 | tf_op jit(solution)/shard_map/psum | solution.py:141
  8.0 30.6 %collective-permute-start = (f32[4,8]{1,0:T(4,128)S(1)}, f32[4,8]{1,0:T(4,128)S(1)}, u32[]{:S(2)}, u32[]{:S(2)}) collective-permute-start(f32[4,8]{1,0:T(4,128)S(1)} %get-tuple-element.90), channel_id=1, source_target_pairs={{0,1},{1,2},{2,3},{3,4},{4,5},{5,6},{6,7},{7,8},{8,9},{9,10},{10,1... | collective-permute-start | bytes 392 | tf_op jit(solution)/shard_map/ppermute | solution.py:22
  12.8 25.1 %copy-start.5 = (f32[16]{0:T(128)S(1)}, f32[16]{0:T(128)}, u32[]{:S(2)}) copy-start(f32[16]{0:T(128)} %param.10) | copy-start | bytes 196
  12.9 25.2 %copy-start.4 = (s32[16,16]{1,0:T(8,128)S(1)}, s32[16,16]{1,0:T(8,128)}, u32[]{:S(2)}) copy-start(s32[16,16]{1,0:T(8,128)} %param.11) | copy-start | bytes 3076
  12.9 25.3 %copy-start.7 = (s32[16]{0:T(128)S(1)}, s32[16]{0:T(128)}, u32[]{:S(2)}) copy-start(s32[16]{0:T(128)} %param.12) | copy-start | bytes 196
  12.9 25.8 %copy-start.3 = (f32[3,16]{1,0:T(4,128)S(1)}, f32[3,16]{1,0:T(4,128)}, u32[]{:S(2)}) copy-start(f32[3,16]{1,0:T(4,128)} %param.9) | copy-start | bytes 580
  12.9 25.7 %collective-permute-start.1 = (f32[4,8]{1,0:T(4,128)S(1)}, f32[4,8]{1,0:T(4,128)S(1)}, u32[]{:S(2)}, u32[]{:S(2)}) collective-permute-start(f32[4,8]{1,0:T(4,128)S(1)} %get-tuple-element.91), channel_id=1, source_target_pairs={{1,0},{2,1},{3,2},{4,3},{5,4},{6,5},{7,6},{8,7},{9,8},{10,9},{11,1... | collective-permute-start | bytes 392 | tf_op jit(solution)/shard_map/ppermute | solution.py:23
  62.0 34.9 %copy-start.6 = (f32[49]{0:T(128)S(1)}, f32[49]{0:T(128)}, u32[]{:S(2)}) copy-start(f32[49]{0:T(128)} %constant.272) | copy-start | bytes 592
  62.0 40.3 %copy-start.8 = (f32[49]{0:T(128)S(1)}, f32[49]{0:T(128)}, u32[]{:S(2)}) copy-start(f32[49]{0:T(128)} %constant.273) | copy-start | bytes 592
  97.4 20.0 %collective-permute-start.2 = (f32[8,16,49]{2,1,0:T(8,128)S(1)}, f32[8,16,49]{2,1,0:T(8,128)S(1)}, u32[]{:S(2)}, u32[]{:S(2)}) collective-permute-start(f32[8,16,49]{2,1,0:T(8,128)S(1)} %get-tuple-element.58), channel_id=1, source_target_pairs={{0,1},{1,2},{2,3},{3,4},{4,5},{5,6},{6,7},{7,8},{8,9},{9,10},{10,1... | collective-permute-start | bytes 75272 | tf_op jit(solution)/shard_map/ppermute | solution.py:22
  100.7 16.6 %collective-permute-start.3 = (f32[8,16,49]{2,1,0:T(8,128)S(1)}, f32[8,16,49]{2,1,0:T(8,128)S(1)}, u32[]{:S(2)}, u32[]{:S(2)}) collective-permute-start(f32[8,16,49]{2,1,0:T(8,128)S(1)} %get-tuple-element.59), channel_id=1, source_target_pairs={{1,0},{2,1},{3,2},{4,3},{5,4},{6,5},{7,6},{8,7},{9,8},{10,9},{11,1... | collective-permute-start | bytes 75272 | tf_op jit(solution)/shard_map/ppermute | solution.py:23
  147.5 6.4 %collective-permute-start.4 = (f32[8,16,49]{2,1,0:T(8,128)S(1)}, f32[8,16,49]{2,1,0:T(8,128)S(1)}, u32[]{:S(2)}, u32[]{:S(2)}) collective-permute-start(f32[8,16,49]{2,1,0:T(8,128)S(1)} %get-tuple-element.56), channel_id=1, source_target_pairs={{0,1},{1,2},{2,3},{3,4},{4,5},{5,6},{6,7},{7,8},{8,9},{9,10},{10,1... | collective-permute-start | bytes 75272 | tf_op jit(solution)/shard_map/ppermute | solution.py:22
  152.1 6.4 %collective-permute-start.5 = (f32[8,16,49]{2,1,0:T(8,128)S(1)}, f32[8,16,49]{2,1,0:T(8,128)S(1)}, u32[]{:S(2)}, u32[]{:S(2)}) collective-permute-start(f32[8,16,49]{2,1,0:T(8,128)S(1)} %get-tuple-element.57), channel_id=1, source_target_pairs={{1,0},{2,1},{3,2},{4,3},{5,4},{6,5},{7,6},{8,7},{9,8},{10,9},{11,1... | collective-permute-start | bytes 75272 | tf_op jit(solution)/shard_map/ppermute | solution.py:23
  159.5 64.3 %copy-start.1 = (bf16[16,256]{1,0:T(8,128)(2,1)S(1)}, bf16[16,256]{1,0:T(8,128)(2,1)}, u32[]{:S(2)}) copy-start(bf16[16,256]{1,0:T(8,128)(2,1)} %param.8) | copy-start | bytes 24580
  188.6 35.2 %copy-start.2 = (f32[16,16,49]{2,1,0:T(8,128)}, f32[16,16,49]{2,1,0:T(8,128)S(1)}, u32[]{:S(2)}) copy-start(f32[16,16,49]{2,1,0:T(8,128)S(1)} %fusion.11) | copy-start | bytes 150532
Sparse Core Ops, SparseCore 0:
  36.8 58.9 all-reduce.1
